TPU v7x, 32 devices: a whole 2x2x4 slice. The times are simulated.
32 devices in a mesh: wide: 4 (over x, core), narrow: 8 (over z, y).
Axes of the slice: x: 2, y: 2, z: 4, core: 2. Of those that a mesh axis runs over, the one named last changes fastest.
Arguments:
- grad_parts: bfloat16 [4, 3584, 8192], P('wide', 'narrow'), may hold values from -6 to 6
- master: bfloat16 [3584, 8192], P('narrow'), may hold values from -0.1875 to 0.1875
- moment_one: float32 [3584, 8192], P('narrow'), may hold values from -4 to 4
- moment_two: float32 [3584, 8192], P('narrow'), may hold values from 0.01 to 1
- gate_up: bfloat16 [3584, 2, 8192], P(None, None, 'narrow'), may hold values from -0.09375 to 0.09375
- tokens: bfloat16 [64, 3584], P(('wide', 'narrow')), may hold values from -6 to 6
- expert_ids: int32 [64, 4], P(('wide', 'narrow')), may hold values from 0 to 7, all different within a row; in each aligned block of 2 rows (0 to 1, 2 to 3, ...) at most 2 rows name the same one
- gate_vals: bfloat16 [64, 4], P(('wide', 'narrow')), may hold values from 0.049804688 to 1
Outputs:
- new_master: bfloat16 [3584, 8192], P('narrow')
- new_one: float32 [3584, 8192], P('narrow')
- new_two: float32 [3584, 8192], P('narrow')
- combined: bfloat16 [64, 3584], P(('wide', 'narrow'))
Inputs may be any that keep to these rules, and one draw needn't show every extreme that they name: `expert_ids`: each token names 4 distinct experts; each device's 2 tokens name every expert at most 2 times (which follows from the distinct ids), and some device names one expert twice.
All inputs are finite; a program needn't handle non-finite values.
Results may differ from a plain program's by a relative error of at most 0.022.
Values may be sent and summed in bfloat16 or wider, within the bound.
No kernel may reach another device: no remote copies, remote signals or barrier semaphores. Data moves between devices by JAX's collectives and lax.ppermute only.
A program may use at most 192 MiB of HBM per device.

v0:
```python
import jax
import jax.numpy as jnp
from jax import lax
from jax.sharding import PartitionSpec as P

EXPERTS = 8
TOPK = 4
QBLOCK = 128
CAP = 2
beta_first = 0.9
beta_second = 0.95
learn_rate = 0.003
adam_eps = 1e-08
quant_limit = 448.0
amax_eps = 1e-06
bias_first = 1.0 - 0.9**10
bias_second = 1.0 - 0.95**10


def adam_quant(grad_sum, master, moment_one, moment_two):
    new_one = beta_first * moment_one + (1.0 - beta_first) * grad_sum
    new_two = beta_second * moment_two + (1.0 - beta_second) * grad_sum * grad_sum
    step_dir = new_one / bias_first / (jnp.sqrt(new_two / bias_second) + adam_eps)
    updated = master.astype(jnp.float32) - learn_rate * step_dir
    row_count, col_count = updated.shape
    blocks = updated.reshape(row_count, col_count // QBLOCK, QBLOCK)
    scales = ((jnp.max(jnp.abs(blocks), axis=2) + amax_eps) / quant_limit).astype(jnp.bfloat16)
    quanta = (
        (blocks / scales.astype(jnp.float32)[:, :, None])
        .astype(jnp.bfloat16)
        .reshape(row_count, col_count)
    )
    return (updated.astype(jnp.bfloat16), new_one, new_two, quanta, scales)


def expert_rows(rows_in, gate_piece, quanta, scales):
    unit_count = gate_piece.shape[2]
    proj_both = jnp.dot(
        rows_in,
        gate_piece.reshape(gate_piece.shape[0], 2 * unit_count),
        preferred_element_type=jnp.float32,
    )
    hidden = (jax.nn.silu(proj_both[:, :unit_count]) * proj_both[:, unit_count:]).astype(
        jnp.bfloat16
    )
    block_count = unit_count // QBLOCK
    per_block = jnp.einsum(
        "rbf,dbf->rbd",
        hidden.reshape(-1, block_count, QBLOCK),
        quanta.reshape(quanta.shape[0], block_count, QBLOCK),
        preferred_element_type=jnp.float32,
    )
    return jnp.einsum("rbd,db->rd", per_block, scales.astype(jnp.float32))


def body(grad_parts, master, moment_one, moment_two, gate_up, tokens, expert_ids, gate_vals):
    grad_sum = lax.psum(grad_parts[0], "wide").astype(jnp.float32)
    new_master, new_one, new_two, quanta, scales = adam_quant(
        grad_sum, master, moment_one, moment_two
    )
    owned_q, owned_s = (
        lax.all_to_all(quanta, "narrow", split_axis=1, concat_axis=0, tiled=True),
        lax.all_to_all(scales, "narrow", split_axis=1, concat_axis=0, tiled=True),
    )
    onehot = (expert_ids[:, :, None] == jnp.arange(EXPERTS, dtype=jnp.int32)[None, None, :]).astype(
        jnp.float32
    )
    gate_float = gate_vals.astype(jnp.float32)
    group_size = lax.axis_size("narrow") // EXPERTS
    tok_count = tokens.shape[0]
    feat_width = tokens.shape[1]
    flat_ids = onehot.reshape(-1, EXPERTS)
    assign_count = flat_ids.shape[0]
    earlier = (jnp.arange(assign_count)[:, None] > jnp.arange(assign_count)[None, :]).astype(
        jnp.float32
    )
    slot_rank = jnp.sum(jnp.dot(earlier, flat_ids) * flat_ids, axis=1)
    slot_hit = (slot_rank[:, None] == jnp.arange(CAP)[None, :].astype(jnp.float32)).astype(
        jnp.float32
    )
    tok_sel = (jnp.arange(assign_count)[:, None] // TOPK == jnp.arange(tok_count)[None, :]).astype(
        jnp.float32
    )
    dispatch_map = jnp.einsum("ae,ac,at->ect", flat_ids, slot_hit, tok_sel)
    combine_weight = jnp.einsum(
        "ae,ac,at->ect", flat_ids * gate_float.reshape(-1)[:, None], slot_hit, tok_sel
    )
    slot_rows = jnp.einsum(
        "ect,td->ecd", dispatch_map.astype(jnp.bfloat16), tokens, preferred_element_type=jnp.float32
    ).astype(jnp.bfloat16)
    outgoing = jnp.repeat(slot_rows, group_size, axis=0)
    received = lax.all_to_all(outgoing, "narrow", split_axis=0, concat_axis=0, tiled=True)
    src_count, slot_count, width_in = received.shape
    partial_value = expert_rows(
        received.reshape(src_count * slot_count, width_in), gate_up, owned_q, owned_s
    )
    partial_value = partial_value.astype(jnp.bfloat16).reshape(src_count, slot_count, width_in)
    returned = lax.all_to_all(partial_value, "narrow", split_axis=0, concat_axis=0, tiled=True)
    summed = jnp.sum(
        returned.astype(jnp.float32).reshape(EXPERTS, group_size, CAP, feat_width), axis=1
    )
    combined = jnp.einsum("ect,ecd->td", combine_weight, summed)
    return (new_master, new_one, new_two, combined.astype(jnp.bfloat16))


def solution(mesh):
    in_specs = (
        P("wide", "narrow", None),
        P("narrow", None),
        P("narrow", None),
        P("narrow", None),
        P(None, None, "narrow"),
        P(("wide", "narrow"), None),
        P(("wide", "narrow"), None),
        P(("wide", "narrow"), None),
    )
    out_specs = (
        P("narrow", None),
        P("narrow", None),
        P("narrow", None),
        P(("wide", "narrow"), None),
    )
    return jax.shard_map(body, mesh=mesh, in_specs=in_specs, out_specs=out_specs, check_vma=False)
```

profile of v0, /device:TPU:0, one launch (start us, length us, event | category | flops | bytes accessed | tf_op | source)
XLA Modules:
  0.0 432.0 jit_solution(17425737134282565379)
XLA Ops:
  7.2 0.7 all-reduce.2.cloned.1.call-update
  7.9 0.8 eq.46
  8.9 0.3 convolution_convert_fusion
  9.2 0.7 copy.32
  10.0 7.3 %all-to-all-start.2 = ((bf16[8,2,3584]{2,1,0:T(2,128)(2,1)}), bf16[8,2,3584]{2,1,0:T(2,128)(2,1)S(1)}, u32[]{:S(2)}, u32[]{:S(2)}) async-start(bf16[8,2,3584]{2,1,0:T(2,128)(2,1)} %copy.32), calls=%async_computation.2 | async-start | bytes 229376 | tf_op jit(solution)/shard_map/all_to_all | solution.py:92
  17.3 132.4 %all-reduce.2.cloned.1.call-done = bf16[448,8192]{1,0:T(8,128)(2,1)} async-done(((bf16[448,8192]{1,0:T(8,128)(2,1)}), bf16[448,8192]{1,0:T(8,128)(2,1)}) %all-reduce.2.cloned.1.call-update) | async-done | bytes 7340048 | tf_op jit(solution)/shard_map/psum | solution.py:57
  149.7 34.3 %abs_bitcast_fusion = (f32[56,8,64,128]{3,1,2,0:T(8,128)}, f32[448,8192]{1,0:T(8,128)}, f32[448,8192]{1,0:T(8,128)}, f32[448,8192]{1,0:T(8,128)}) fusion(bf16[448,8192]{1,0:T(8,128)(2,1)} %param.9, bf16[448,8192]{1,0:T(8,128)(2,1)} %all-reduce.2.cloned.1.call-done, f32[448,8192]{1,0:T(8,128)} %param.10, f32[448,8192]{1,0:T(8,128)} %param.11), kind=kLoop, calls=%fused_computation.6 | loop fusion | flops 58720256 | bytes 102760448
  184.0 13.6 %copy.49 = f32[56,8,64,128]{3,2,1,0:T(8,128)} copy(f32[56,8,64,128]{3,1,2,0:T(8,128)} %get-tuple-element.4) | data formatting | bytes 29360128
  197.6 9.0 %reduce_max.9 = f32[448,64]{1,0:T(8,128)S(1)} reduce(f32[448,64,128]{2,1,0:T(8,128)} %bitcast.68, f32[]{:T(128)} %constant.46.clone.1), dimensions={2}, to_apply=%region_2.0 | reduce | flops 3641344 | bytes 14794756 | tf_op jit(solution)/shard_map/reduce_max | solution.py:27
  206.8 0.6 fusion.23
  207.6 5.5 %all-to-all-start = ((bf16[448,8,8]{0,2,1:T(8,128)(2,1)}), bf16[448,8,8]{0,2,1:T(8,128)(2,1)S(1)}, u32[]{:S(2)}, u32[]{:S(2)}) async-start(bf16[448,8,8]{0,2,1:T(8,128)(2,1)} %get-tuple-element.10), calls=%async_computation | async-start | bytes 131072 | tf_op jit(solution)/shard_map/all_to_all | solution.py:63
  213.1 4.0 div.53
  217.2 18.6 %fusion.2 = (bf16[448,8192]{1,0:T(8,128)(2,1)S(1)}, bf16[448,8192]{1,0:T(8,128)(2,1)}) fusion(f32[448,8192]{1,0:T(8,128)} %get-tuple-element.5, f32[56,8,64,128]{3,2,1,0:T(8,128)S(1)} %bitcast.69), kind=kLoop, calls=%fused_computation.5 | loop fusion | flops 11010048 | bytes 44040192 | tf_op jit(solution)/shard_map/convert_element_type | solution.py:30
  235.7 4.1 copy.69
  239.9 6.0 %all-to-all-start.1 = ((bf16[448,8,1024]{2,0,1:T(8,128)(2,1)}), bf16[448,8,1024]{2,0,1:T(8,128)(2,1)}, u32[]{:S(2)}, u32[]{:S(2)}) async-start(bf16[448,8,1024]{2,0,1:T(8,128)(2,1)} %bitcast.70), calls=%async_computation.1 | async-start | bytes 14680064 | tf_op jit(solution)/shard_map/all_to_all | solution.py:62
  245.9 16.1 %copy.52 = bf16[448,8,2,1024]{3,1,2,0:T(8,128)(2,1)} copy(bf16[448,8,2,1024]{3,2,1,0:T(2,128)(2,1)} %bitcast.72) | data formatting | bytes 29360128
  262.0 7.2 %fusion.57 = f32[16,2048]{1,0:T(8,128)S(1)} fusion(bf16[16,3584]{1,0:T(8,128)(2,1)S(1)} %reshape.99, bf16[3584,2048]{1,0:T(8,128)(2,1)} %bitcast.67), kind=kOutput, calls=%fused_computation.57 | convolution fusion | flops 234881024 | bytes 14925824 | tf_op jit(solution)/shard_map/dot_general | solution.py:38
  269.3 136.2 %all-to-all-done.1 = bf16[448,8,1024]{2,0,1:T(8,128)(2,1)} async-done(((bf16[448,8,1024]{2,0,1:T(8,128)(2,1)}), bf16[448,8,1024]{2,0,1:T(8,128)(2,1)}, u32[]{:S(2)}, u32[]{:S(2)}) %all-to-all-start.1) | async-done | bytes 7340064 | tf_op jit(solution)/shard_map/all_to_all | solution.py:62
  405.6 5.0 %copy.51 = bf16[448,8,8,128]{3,2,1,0:T(8,128)(2,1)S(1)} copy(bf16[448,8,8,128]{3,1,2,0:T(8,128)(2,1)} %bitcast.24) | data formatting | bytes 14680064
  410.5 2.1 fusion.12
  412.6 0.7 reshape.102
  413.3 3.6 all-to-all-start.3
  417.0 7.1 %all-to-all-done.3 = bf16[8,2,3584]{2,1,0:T(2,128)(2,1)S(1)} async-done(((bf16[8,2,3584]{2,1,0:T(2,128)(2,1)}), bf16[8,2,3584]{2,1,0:T(2,128)(2,1)S(1)}, u32[]{:S(2)}, u32[]{:S(2)}) %all-to-all-start.3) | async-done | bytes 114720 | tf_op jit(solution)/shard_map/all_to_all | solution.py:98
  424.2 0.9 fusion.11
  (20 shorter events, 0.8 us)
Async XLA Ops:
  7.2 1.7 copy-start
  7.2 142.6 %all-reduce.2.cloned.1.call-start = ((), (), s32[]{:S(2)}) async-start(), calls=%async_computation.4 | async-start | bytes 14680064 | tf_op jit(solution)/shard_map/psum | solution.py:57
  10.0 197.6 %all-to-all-start.2 = ((bf16[8,2,3584]{2,1,0:T(2,128)(2,1)}), bf16[8,2,3584]{2,1,0:T(2,128)(2,1)S(1)}, u32[]{:S(2)}, u32[]{:S(2)}) async-start(bf16[8,2,3584]{2,1,0:T(2,128)(2,1)} %copy.32), calls=%async_computation.2 | async-start | bytes 229376 | tf_op jit(solution)/shard_map/all_to_all | solution.py:92
  207.6 32.3 %all-to-all-start = ((bf16[448,8,8]{0,2,1:T(8,128)(2,1)}), bf16[448,8,8]{0,2,1:T(8,128)(2,1)S(1)}, u32[]{:S(2)}, u32[]{:S(2)}) async-start(bf16[448,8,8]{0,2,1:T(8,128)(2,1)} %get-tuple-element.10), calls=%async_computation | async-start | bytes 131072 | tf_op jit(solution)/shard_map/all_to_all | solution.py:63
  239.9 165.7 %all-to-all-start.1 = ((bf16[448,8,1024]{2,0,1:T(8,128)(2,1)}), bf16[448,8,1024]{2,0,1:T(8,128)(2,1)}, u32[]{:S(2)}, u32[]{:S(2)}) async-start(bf16[448,8,1024]{2,0,1:T(8,128)(2,1)} %bitcast.70), calls=%async_computation.1 | async-start | bytes 14680064 | tf_op jit(solution)/shard_map/all_to_all | solution.py:62
  262.0 163.1 %copy-start.1 = (bf16[2,3584]{1,0:T(2,128)(2,1)S(1)}, bf16[2,3584]{1,0:T(2,128)(2,1)}, u32[]{:S(2)}) copy-start(bf16[2,3584]{1,0:T(2,128)(2,1)} %param.13) | copy-start | bytes 43012
  269.2 147.8 %copy-start.2 = (bf16[2,4]{1,0:T(2,128)(2,1)S(1)}, bf16[2,4]{1,0:T(2,128)(2,1)}, u32[]{:S(2)}) copy-start(bf16[2,4]{1,0:T(2,128)(2,1)} %param.15) | copy-start | bytes 52
  413.3 10.9 %all-to-all-start.3 = ((bf16[8,2,3584]{2,1,0:T(2,128)(2,1)}), bf16[8,2,3584]{2,1,0:T(2,128)(2,1)S(1)}, u32[]{:S(2)}, u32[]{:S(2)}) async-start(bf16[8,2,3584]{2,1,0:T(2,128)(2,1)} %reshape.102), calls=%async_computation.3 | async-start | bytes 229376 | tf_op jit(solution)/shard_map/all_to_all | solution.py:98
Sparse Core Ops, SparseCore 0:
  10.4 139.3 all-reduce.1
where the time goes:
time: 433 us; the launch traced here: 432 us
  waiting for transfers between devices  276 us (64%)
  other arithmetic  62.6 us (14%)
  local copies, waits for them, and re-layouts  45.6 us (11%)
  starting transfers between devices  22.5 us (5%)
  between operations  14.1 us (3%)
  matrix products  10.7 us (2%)
    all_to_all x1, waiting for transfers between devices, body(): lax.all_to_all(quanta, 'narrow', split_axis=1, concat_axis=0, tiled=True)  136 us
    psum x1, waiting for transfers between devices, body(): grad_sum = lax.psum(grad_parts[0], 'wide').astype(jnp.float32)  132 us
    unnamed x9, local copies, waits for them, and re-layouts  34.7 us
    unnamed x2, other arithmetic  34.3 us
    convert_element_type x1, other arithmetic, adam_quant(): quanta = (blocks / scales.astype(jnp.float32)[:, :, None]).astype(jnp.bfl...  18.6 us
    reduce_max x1, other arithmetic, adam_quant(): jnp.max(jnp.abs(blocks), axis=2) + amax_eps  9.03 us
  transfers between devices with their start and end apart: 5, of which 3 were waited for; matrix products, arithmetic and copies ran while one was open for 25% of the time, Pallas kernels for 0%

commit v1 on v0

--- a/solution.py
+++ b/solution.py
@@ -54,7 +54,7 @@
 
 
 def body(grad_parts, master, moment_one, moment_two, gate_up, tokens, expert_ids, gate_vals):
-    grad_sum = lax.psum(grad_parts[0], "wide").astype(jnp.float32)
+    grad_sum = jnp.sum(lax.all_gather(grad_parts[0], "wide"), axis=0).astype(jnp.float32)
     new_master, new_one, new_two, quanta, scales = adam_quant(
         grad_sum, master, moment_one, moment_two
     )

time: 433 us -> 489 us (1.13)
  waiting for transfers between devices: 276 us -> 318 us
  other arithmetic: 62.6 us -> 77.3 us
    all_gather x0 -> x1, waiting for transfers between devices: none -> 173 us  [body(): lax.all_gather(grad_parts[0], 'wide')]
    psum x1 -> x0, waiting for transfers between devices: 132 us -> none  [body(): grad_sum = lax.psum(grad_parts[0], 'wide').astype(jnp.float32)]
    reduce_sum x0 -> x1, other arithmetic: none -> 14.7 us  [body(): jnp.sum(lax.all_gather(grad_parts[0], 'wide'), axis=0).astype(jnp.float32)]
  transfers between devices with their start and end apart: 5 -> 5, of which waited for: 3 -> 3; matrix products, arithmetic and copies ran while one was open for 25% -> 26% of each run, Pallas kernels for 0% -> 0%
where the time goes in v1:
time: 489 us; the launch traced here: 488 us
  waiting for transfers between devices  318 us (65%)
  other arithmetic  77.3 us (16%)
  local copies, waits for them, and re-layouts  45.6 us (9%)
  starting transfers between devices  22.5 us (5%)
  between operations  14.1 us (3%)
  matrix products  10.7 us (2%)
    all_gather x1, waiting for transfers between devices, body(): lax.all_gather(grad_parts[0], 'wide')  173 us
    all_to_all x1, waiting for transfers between devices, body(): lax.all_to_all(quanta, 'narrow', split_axis=1, concat_axis=0, tiled=True)  137 us
    unnamed x9, local copies, waits for them, and re-layouts  34.7 us
    unnamed x2, other arithmetic  34.3 us
    convert_element_type x1, other arithmetic, adam_quant(): quanta = (blocks / scales.astype(jnp.float32)[:, :, None]).astype(jnp.bfl...  18.6 us
    reduce_sum x1, other arithmetic, body(): jnp.sum(lax.all_gather(grad_parts[0], 'wide'), axis=0).astype(jnp.float32)  14.7 us
  transfers between devices with their start and end apart: 5, of which 3 were waited for; matrix products, arithmetic and copies ran while one was open for 26% of the time, Pallas kernels for 0%

profile of v1, /device:TPU:0, one launch (start us, length us, event | category | flops | bytes accessed | tf_op | source)
XLA Modules:
  0.0 488.1 jit_solution(4888091112879184035)
XLA Ops:
  7.2 0.7 all-gather.2.cloned.1.call-update
  7.9 0.8 eq.46
  9.2 0.7 copy.32
  10.0 7.3 %all-to-all-start.2 = ((bf16[8,2,3584]{2,1,0:T(2,128)(2,1)}), bf16[8,2,3584]{2,1,0:T(2,128)(2,1)S(1)}, u32[]{:S(2)}, u32[]{:S(2)}) async-start(bf16[8,2,3584]{2,1,0:T(2,128)(2,1)} %copy.32), calls=%async_computation.2 | async-start | bytes 229376 | tf_op jit(solution)/shard_map/all_to_all | solution.py:92
  17.3 173.0 %all-gather.2.cloned.1.call-done = bf16[4,448,8192]{2,1,0:T(8,128)(2,1)} async-done(((bf16[1,448,8192]{2,1,0:T(8,128)(2,1)}), bf16[4,448,8192]{2,1,0:T(8,128)(2,1)}) %all-gather.2.cloned.1.call-update) | async-done | bytes 29360144 | tf_op jit(solution)/shard_map/all_gather | solution.py:57
  190.3 14.7 %reduce_sum.25 = bf16[448,8192]{1,0:T(8,128)(2,1)} reduce(bf16[4,448,8192]{2,1,0:T(8,128)(2,1)} %all-gather.2.cloned.1.call-done, bf16[]{:T(256)} %constant.34.clone.1), dimensions={0}, to_apply=%region_0.0 | reduce | flops 11010048 | bytes 36700160 | tf_op jit(solution)/shard_map/reduce_sum | solution.py:57
  205.0 34.3 %abs_bitcast_fusion = (f32[56,8,64,128]{3,1,2,0:T(8,128)}, f32[448,8192]{1,0:T(8,128)}, f32[448,8192]{1,0:T(8,128)}, f32[448,8192]{1,0:T(8,128)}) fusion(bf16[448,8192]{1,0:T(8,128)(2,1)} %param.9, bf16[448,8192]{1,0:T(8,128)(2,1)} %reduce_sum.25, f32[448,8192]{1,0:T(8,128)} %param.10, f32[448,8192]{1,0:T(8,128)} %param.11), kind=kLoop, calls=%fused_computation.6 | loop fusion | flops 58720256 | bytes 102760448
  239.3 13.6 %copy.49 = f32[56,8,64,128]{3,2,1,0:T(8,128)} copy(f32[56,8,64,128]{3,1,2,0:T(8,128)} %get-tuple-element.4) | data formatting | bytes 29360128
  252.9 9.0 %reduce_max.9 = f32[448,64]{1,0:T(8,128)S(1)} reduce(f32[448,64,128]{2,1,0:T(8,128)} %bitcast.67, f32[]{:T(128)} %constant.48.clone.1), dimensions={2}, to_apply=%region_2.0 | reduce | flops 3641344 | bytes 14794756 | tf_op jit(solution)/shard_map/reduce_max | solution.py:27
  262.1 0.6 fusion.23
  262.9 5.5 %all-to-all-start = ((bf16[448,8,8]{0,2,1:T(8,128)(2,1)}), bf16[448,8,8]{0,2,1:T(8,128)(2,1)S(1)}, u32[]{:S(2)}, u32[]{:S(2)}) async-start(bf16[448,8,8]{0,2,1:T(8,128)(2,1)} %get-tuple-element.10), calls=%async_computation | async-start | bytes 131072 | tf_op jit(solution)/shard_map/all_to_all | solution.py:63
  268.4 4.0 div.53
  272.5 18.6 %fusion.2 = (bf16[448,8192]{1,0:T(8,128)(2,1)S(1)}, bf16[448,8192]{1,0:T(8,128)(2,1)}) fusion(f32[448,8192]{1,0:T(8,128)} %get-tuple-element.5, f32[56,8,64,128]{3,2,1,0:T(8,128)S(1)} %bitcast.68), kind=kLoop, calls=%fused_computation.5 | loop fusion | flops 11010048 | bytes 44040192 | tf_op jit(solution)/shard_map/convert_element_type | solution.py:30
  291.0 4.1 copy.69
  295.2 6.0 %all-to-all-start.1 = ((bf16[448,8,1024]{2,0,1:T(8,128)(2,1)}), bf16[448,8,1024]{2,0,1:T(8,128)(2,1)}, u32[]{:S(2)}, u32[]{:S(2)}) async-start(bf16[448,8,1024]{2,0,1:T(8,128)(2,1)} %bitcast.69), calls=%async_computation.1 | async-start | bytes 14680064 | tf_op jit(solution)/shard_map/all_to_all | solution.py:62
  301.2 16.1 %copy.52 = bf16[448,8,2,1024]{3,1,2,0:T(8,128)(2,1)} copy(bf16[448,8,2,1024]{3,2,1,0:T(2,128)(2,1)} %bitcast.71) | data formatting | bytes 29360128
  317.3 7.2 %fusion.57 = f32[16,2048]{1,0:T(8,128)S(1)} fusion(bf16[16,3584]{1,0:T(8,128)(2,1)S(1)} %reshape.99, bf16[3584,2048]{1,0:T(8,128)(2,1)} %bitcast.66), kind=kOutput, calls=%fused_computation.57 | convolution fusion | flops 234881024 | bytes 14925824 | tf_op jit(solution)/shard_map/dot_general | solution.py:38
  324.6 137.1 %all-to-all-done.1 = bf16[448,8,1024]{2,0,1:T(8,128)(2,1)} async-done(((bf16[448,8,1024]{2,0,1:T(8,128)(2,1)}), bf16[448,8,1024]{2,0,1:T(8,128)(2,1)}, u32[]{:S(2)}, u32[]{:S(2)}) %all-to-all-start.1) | async-done | bytes 7340064 | tf_op jit(solution)/shard_map/all_to_all | solution.py:62
  461.7 5.0 %copy.51 = bf16[448,8,8,128]{3,2,1,0:T(8,128)(2,1)S(1)} copy(bf16[448,8,8,128]{3,1,2,0:T(8,128)(2,1)} %bitcast.23) | data formatting | bytes 14680064
  466.7 2.1 fusion.12
  468.8 0.7 reshape.102
  469.5 3.6 all-to-all-start.3
  473.2 7.1 %all-to-all-done.3 = bf16[8,2,3584]{2,1,0:T(2,128)(2,1)S(1)} async-done(((bf16[8,2,3584]{2,1,0:T(2,128)(2,1)}), bf16[8,2,3584]{2,1,0:T(2,128)(2,1)S(1)}, u32[]{:S(2)}, u32[]{:S(2)}) %all-to-all-start.3) | async-done | bytes 114720 | tf_op jit(solution)/shard_map/all_to_all | solution.py:98
  480.3 0.9 fusion.11
  (21 shorter events, 1.1 us)
Async XLA Ops:
  7.2 1.7 copy-start
  7.2 183.1 %all-gather.2.cloned.1.call-start = ((), (), s32[]{:S(2)}) async-start(), calls=%async_computation.4 | async-start | bytes 36700160 | tf_op jit(solution)/shard_map/all_gather | solution.py:57
  10.0 252.9 %all-to-all-start.2 = ((bf16[8,2,3584]{2,1,0:T(2,128)(2,1)}), bf16[8,2,3584]{2,1,0:T(2,128)(2,1)S(1)}, u32[]{:S(2)}, u32[]{:S(2)}) async-start(bf16[8,2,3584]{2,1,0:T(2,128)(2,1)} %copy.32), calls=%async_computation.2 | async-start | bytes 229376 | tf_op jit(solution)/shard_map/all_to_all | solution.py:92
  262.9 32.3 %all-to-all-start = ((bf16[448,8,8]{0,2,1:T(8,128)(2,1)}), bf16[448,8,8]{0,2,1:T(8,128)(2,1)S(1)}, u32[]{:S(2)}, u32[]{:S(2)}) async-start(bf16[448,8,8]{0,2,1:T(8,128)(2,1)} %get-tuple-element.10), calls=%async_computation | async-start | bytes 131072 | tf_op jit(solution)/shard_map/all_to_all | solution.py:63
  295.2 166.6 %all-to-all-start.1 = ((bf16[448,8,1024]{2,0,1:T(8,128)(2,1)}), bf16[448,8,1024]{2,0,1:T(8,128)(2,1)}, u32[]{:S(2)}, u32[]{:S(2)}) async-start(bf16[448,8,1024]{2,0,1:T(8,128)(2,1)} %bitcast.69), calls=%async_computation.1 | async-start | bytes 14680064 | tf_op jit(solution)/shard_map/all_to_all | solution.py:62
  317.3 164.0 %copy-start.1 = (bf16[2,3584]{1,0:T(2,128)(2,1)S(1)}, bf16[2,3584]{1,0:T(2,128)(2,1)}, u32[]{:S(2)}) copy-start(bf16[2,3584]{1,0:T(2,128)(2,1)} %param.13) | copy-start | bytes 43012
  324.5 148.6 %copy-start.2 = (bf16[2,4]{1,0:T(2,128)(2,1)S(1)}, bf16[2,4]{1,0:T(2,128)(2,1)}, u32[]{:S(2)}) copy-start(bf16[2,4]{1,0:T(2,128)(2,1)} %param.15) | copy-start | bytes 52
  469.5 10.9 %all-to-all-start.3 = ((bf16[8,2,3584]{2,1,0:T(2,128)(2,1)}), bf16[8,2,3584]{2,1,0:T(2,128)(2,1)S(1)}, u32[]{:S(2)}, u32[]{:S(2)}) async-start(bf16[8,2,3584]{2,1,0:T(2,128)(2,1)} %reshape.102), calls=%async_computation.3 | async-start | bytes 229376 | tf_op jit(solution)/shard_map/all_to_all | solution.py:98
Sparse Core Ops, SparseCore 0:
  9.6 180.6 all-gather.1
